TPU v7x, 128 devices: a whole 4x4x4 slice. The times are simulated.
128 devices in a mesh: users: 4 (over z_lo, core), items: 32 (over x, y, z_hi).
Axes of the slice: x: 4, y: 4, z: 4 (z_hi: 2, z_lo: 2; z = z_hi * 2 + z_lo), core: 2. Of those that a mesh axis runs over, the one named last changes fastest.
Arguments:
- user_factors: float32 [16384, 128], P(('users', 'items')), may hold values from -1.8 to 1.8
- item_factors: float32 [65536, 128], P(('items', 'users')), may hold values from -1.8 to 1.8
- block_coords: int32 [4, 32, 256, 2], P('users', 'items'), may hold values from 0 to 31, as said below
- block_counts: int32 [4, 32], P('users', 'items'), may hold values from 32 to 256, as said below
- ratings: bfloat16 [4, 32, 256, 128, 128], P('users', 'items'), may hold values from -6 to 6
- weights: bfloat16 [4, 32, 256, 128, 128], P('users', 'items'), may hold values from 0 to 2, as said below
Outputs:
- new_users: float32 [16384, 128], P(('users', 'items'))
- new_items: float32 [65536, 128], P(('items', 'users'))
Inputs may be any that keep to these rules, and one draw needn't show every extreme that they name: `block_coords`: within one group and shard the 256 slots name distinct pairs of user block and item block, also the slots that are not live. `block_counts`: some group and shard has all 256 slots live in every draw. `weights`: zero marks an unobserved rating.
All inputs are finite; a program needn't handle non-finite values.
Results may differ from a plain program's by a relative error of at most 0.002.
Values may be sent and summed in bfloat16 or wider, within the bound.
A program may use at most 192 MiB of HBM per device.

v0:
```python
import functools

import jax
import jax.numpy as jnp
from jax import lax
from jax.experimental import pallas as pl
from jax.experimental.pallas import tpu as pltpu
from jax.sharding import PartitionSpec as P

BF = jnp.bfloat16
F32 = jnp.float32
MESH = pl.DeviceIdType.MESH

TILE = 128
RANK = 128
STEPS = 2
SLOTS = 256
ITEM_BLOCKS = 16
USER_RATE = 20.0 / 65536
ITEM_RATE = 20.0 / 16384


def contract(a, b, da, db):
    return lax.dot_general(a, b, (((da,), (db,)), ((), ())), preferred_element_type=F32)


def kernel(
    users_ref, items_ref, coords_ref, counts_ref, ratings_hbm, weights_hbm,
    new_users_ref, new_items_ref,
    ratings, weights, table_v, table_s,
    user_tab, item_tab, user_pair, user_master, item_master,
    grad_send, grad_own, ring_far, near_send, ring_near, pair_send, pair_recv,
    item_grad, core_send, core_recv, item_sum, zl_send, zl_recv,
    load_sem, pair_ss, pair_rs, agn_ss, agn_rs, agf_ss, agf_rs, rsf_ss, rsf_rs,
    rsn_ss, rsn_rs, core_ss, core_rs, zl_ss, zl_rs, agi_ss, agi_rs,
):
    me_u = lax.axis_index("users")
    me_i = lax.axis_index("items")
    core = me_u % 2
    zlo = me_u // 2
    x = me_i // 8
    y = (me_i // 2) % 4
    zh = me_i % 2
    near = x + core * (y - x)
    far = y + core * (x - y)
    near_stride = 8 - 6 * core
    far_stride = 2 + 6 * core

    def near_peer(r):
        return (me_u, me_i + ((near + r) % 4 - near) * near_stride)

    def far_peer(r):
        return (me_u, me_i + ((far + r) % 4 - far) * far_stride)

    pair_peer = (me_u, me_i + 1 - 2 * zh)
    core_peer = (me_u + 1 - 2 * core, me_i)
    zlo_peer = (me_u + 2 - 4 * zlo, me_i)

    def remote(src, dst, ss, rs, peer):
        return pltpu.make_async_remote_copy(
            src_ref=src, dst_ref=dst, send_sem=ss, recv_sem=rs, device_id=peer, device_id_type=MESH
        )

    loads = (
        pltpu.make_async_copy(ratings_hbm.at[0, 0], ratings.at[pl.ds(0, SLOTS)], load_sem.at[0]),
        pltpu.make_async_copy(weights_hbm.at[0, 0], weights.at[pl.ds(0, SLOTS)], load_sem.at[1]),
    )
    for copy in loads:
        copy.start()

    peers = [near_peer(r) for r in (1, 2, 3)] + [far_peer(r) for r in (1, 2, 3)]
    peers += [pair_peer, core_peer, zlo_peer]
    barrier = pltpu.get_barrier_semaphore()
    for peer in peers:
        pl.semaphore_signal(barrier, inc=1, device_id=peer, device_id_type=MESH)
    pl.semaphore_wait(barrier, len(peers))

    def pair_copy(step):
        if step == 0:
            return remote(users_ref, user_pair, pair_ss.at[0], pair_rs.at[0], pair_peer)
        if step == 1:
            return remote(pair_send.at[0], pair_recv.at[0], pair_ss.at[1], pair_rs.at[1], pair_peer)
        return remote(
            pair_send.at[1, 1 - zh], pair_recv.at[1, 1 - zh], pair_ss.at[2], pair_rs.at[2], pair_peer
        )

    def gather_near(step, r):
        piece = user_tab.at[step, far, near]
        return remote(piece, piece, agn_ss.at[step, r - 1], agn_rs.at[step, r - 1], near_peer(r))

    def gather_far(step, r, n):
        piece = user_tab.at[step, far, n]
        return remote(piece, piece, agf_ss.at[step, r - 1, n], agf_rs.at[step, r - 1, n], far_peer(r))

    def reduce_far(step, r, h):
        return remote(
            grad_send.at[step, r - 1, h], ring_far.at[step, r - 1, h],
            rsf_ss.at[step, r - 1, h], rsf_rs.at[step, r - 1, h], far_peer(r),
        )

    def reduce_near(step, r):
        return remote(
            near_send.at[step, (near + r) % 4], ring_near.at[step, r - 1],
            rsn_ss.at[step, r - 1], rsn_rs.at[step, r - 1], near_peer(r),
        )

    def reduce_core(step):
        return remote(core_send.at[step], core_recv.at[step], core_ss.at[step], core_rs.at[step], core_peer)

    def reduce_zlo(step):
        return remote(zl_send.at[step], zl_recv.at[step], zl_ss.at[step], zl_rs.at[step], zlo_peer)

    def gather_items(step, k):
        quarter = me_u if k < 2 else me_u + 2 - 4 * zlo
        piece = item_tab.at[step, quarter]
        return remote(
            piece, piece, agi_ss.at[step, k], agi_rs.at[step, k], zlo_peer if k == 0 else core_peer
        )

    def send_users(step):
        for r in (1, 3, 2):
            gather_near(step, r).start()
        for r in (1, 3, 2):
            gather_far(step, r, near).start()

    def forward_users(step, r):
        gather_near(step, r).wait_recv()
        n = (near + 4 - r) % 4
        for k in (1, 3, 2):
            gather_far(step, k, n).start()

    def send_items(step):
        gather_items(step, 0).start()
        gather_items(step, 1).start()

    pair_copy(0).start()
    item_master[...] = items_ref[...]
    item_tab[0, me_u] = items_ref[...].astype(BF)
    send_items(0)

    coords = coords_ref[0, 0]
    cell = coords[:, 0:1] * ITEM_BLOCKS + coords[:, 1:2]
    slot = lax.broadcasted_iota(jnp.int32, (SLOTS, 512), 0)
    hit = (cell == lax.broadcasted_iota(jnp.int32, (SLOTS, 512), 1)) & (slot < counts_ref[0, 0])
    table_v[...] = SLOTS + jnp.sum(jnp.where(hit, slot - SLOTS, 0), axis=0, keepdims=True)
    to_scalars = pltpu.make_async_copy(table_v, table_s, load_sem.at[2])
    to_scalars.start()
    ratings[SLOTS] = jnp.zeros((TILE, TILE), BF)
    weights[SLOTS] = jnp.zeros((TILE, TILE), BF)

    pair_copy(0).wait_recv()
    user_master[zh] = users_ref[...]
    user_master[1 - zh] = user_pair[...]
    user_tab[0, far, near] = user_master[...].astype(BF)
    send_users(0)
    to_scalars.wait()

    own_half = near // 2
    mate = 3 - 2 * (near % 2)

    for step in range(STEPS):
        gather_items(step, 0).wait_recv()
        gather_items(step, 2).start()
        gather_items(step, 1).wait_recv()
        if step == 0:
            for copy in loads:
                copy.wait()
        gather_items(step, 2).wait_recv()
        item_grad[...] = jnp.zeros_like(item_grad)

        def part(c, carry):
            rel = ((c + 1) // 2) % 4
            flip = (c + 1) % 2

            @pl.when(c == 0)
            def _():
                forward_users(step, mate)

            @pl.when(c == 1)
            def _():
                forward_users(step, 2)
                forward_users(step, 4 - mate)

            half = jnp.where(rel == 0, (own_half + 1 + flip) % 2, (own_half + flip) % 2)
            chunk = (far + rel) % 4

            @pl.when(rel > 0)
            def _():
                for k in range(2):
                    gather_far(step, 4 - rel, 2 * half + k).wait_recv()

            u = user_tab[step, chunk, pl.ds(2 * half, 2)].reshape(4 * TILE, RANK)
            v = item_tab[step].reshape(ITEM_BLOCKS * TILE, RANK)
            scores = contract(u, v, 1, 1)
            rows = []
            for a in range(4):
                block = (2 * half + a // 2) * near_stride + chunk * far_stride + a % 2
                cols = []
                for b in range(ITEM_BLOCKS):
                    k = table_s[0, block * ITEM_BLOCKS + b]
                    score = scores[a * TILE:(a + 1) * TILE, b * TILE:(b + 1) * TILE]
                    err = weights[k].astype(F32) * (score - ratings[k].astype(F32))
                    cols.append(err.astype(BF))
                rows.append(jnp.concatenate(cols, axis=1))
            errors = jnp.concatenate(rows, axis=0)
            user_part = contract(errors, v, 1, 0)
            item_part = contract(u, errors, 0, 0)
            for q in range(4):
                item_grad[q] += item_part[:, q * 512:(q + 1) * 512]

            @pl.when(rel == 0)
            def _():
                grad_own[half] = user_part

            @pl.when(rel > 0)
            def _():
                grad_send[step, rel - 1, half] = user_part.astype(BF)
                reduce_far(step, rel, half).start()

            return carry

        lax.fori_loop(0, 8, part, 0)

        for z in range(2):
            core_send[step, z] = item_grad[2 * z + 1 - core].astype(BF)
        reduce_core(step).start()

        for h in range(2):
            for r in (1, 2, 3):
                reduce_far(step, r, h).wait_recv()
            total = grad_own[h]
            for r in range(3):
                total = total + ring_far[step, r, h].astype(F32)
            grad_own[h] = total
            near_send[step, pl.ds(2 * h, 2)] = total.astype(BF).reshape(2, 2 * TILE, RANK)
        for r in (1, 3, 2):
            reduce_near(step, r).start()

        reduce_core(step).wait_recv()
        for z in range(2):
            item_sum[z] = item_grad[2 * z + core] + core_recv[step, z].astype(F32)
        zl_send[step] = item_sum[1 - zlo].astype(BF)
        reduce_zlo(step).start()

        for r in (1, 2, 3):
            reduce_near(step, r).wait_recv()
        total = grad_own[near // 2, pl.ds(pl.multiple_of((near % 2) * 256, 256), 256)]
        for r in range(3):
            total = total + ring_near[step, r].astype(F32)
        pair_send[step] = total.astype(BF).reshape(2, TILE, RANK)
        pair_copy(step + 1).start()

        reduce_zlo(step).wait_recv()
        item_total = (item_sum[zlo] + zl_recv[step].astype(F32)).T
        new_rows = item_master[...] - ITEM_RATE * item_total
        if step + 1 < STEPS:
            item_master[...] = new_rows
            item_tab[step + 1, me_u] = new_rows.astype(BF)
            send_items(step + 1)
        else:
            new_items_ref[...] = new_rows

        pair_copy(step + 1).wait_recv()
        if step + 1 < STEPS:
            both = pair_send[step].astype(F32) + pair_recv[step].astype(F32)
            user_master[...] = user_master[...] - USER_RATE * both
            user_tab[step + 1, far, near] = user_master[...].astype(BF)
            send_users(step + 1)
        else:
            grad_own[0, 0:256] = total
            mine = grad_own[0, pl.ds(pl.multiple_of(zh * TILE, TILE), TILE)]
            mine = mine + pair_recv[step, zh].astype(F32)
            new_users_ref[...] = user_master[zh] - USER_RATE * mine

    for step in range(STEPS):
        for r in (1, 2, 3):
            gather_near(step, r).wait_send()
            for n in range(4):
                gather_far(step, r, n).wait_send()
            for h in range(2):
                reduce_far(step, r, h).wait_send()
            reduce_near(step, r).wait_send()
        reduce_core(step).wait_send()
        reduce_zlo(step).wait_send()
        for k in range(3):
            gather_items(step, k).wait_send()
    for step in range(STEPS + 1):
        pair_copy(step).wait_send()


def per_device(users, items, coords, counts, ratings, weights):
    vmem = pl.BlockSpec(memory_space=pltpu.VMEM)
    hbm = pl.BlockSpec(memory_space=pl.ANY)
    dma = pltpu.SemaphoreType.DMA
    return pl.pallas_call(
        kernel,
        name="factorize",
        out_shape=(
            jax.ShapeDtypeStruct(users.shape, F32),
            jax.ShapeDtypeStruct(items.shape, F32),
        ),
        in_specs=[vmem, vmem, vmem, pl.BlockSpec(memory_space=pltpu.SMEM), hbm, hbm],
        out_specs=(vmem, vmem),
        scratch_shapes=[
            pltpu.VMEM((SLOTS + 1, TILE, TILE), BF),
            pltpu.VMEM((SLOTS + 1, TILE, TILE), BF),
            pltpu.VMEM((1, 512), jnp.int32),
            pltpu.SMEM((1, 512), jnp.int32),
            pltpu.VMEM((STEPS, 4, 4, 2, TILE, RANK), BF),
            pltpu.VMEM((STEPS, 4, 512, RANK), BF),
            pltpu.VMEM((TILE, RANK), F32),
            pltpu.VMEM((2, TILE, RANK), F32),
            pltpu.VMEM((512, RANK), F32),
            pltpu.VMEM((STEPS, 3, 2, 512, RANK), BF),
            pltpu.VMEM((2, 512, RANK), F32),
            pltpu.VMEM((STEPS, 3, 2, 512, RANK), BF),
            pltpu.VMEM((STEPS, 4, 256, RANK), BF),
            pltpu.VMEM((STEPS, 3, 256, RANK), BF),
            pltpu.VMEM((STEPS, 2, TILE, RANK), BF),
            pltpu.VMEM((STEPS, 2, TILE, RANK), BF),
            pltpu.VMEM((4, RANK, 512), F32),
            pltpu.VMEM((STEPS, 2, RANK, 512), BF),
            pltpu.VMEM((STEPS, 2, RANK, 512), BF),
            pltpu.VMEM((2, RANK, 512), F32),
            pltpu.VMEM((STEPS, RANK, 512), BF),
            pltpu.VMEM((STEPS, RANK, 512), BF),
            dma((3,)),
            dma((STEPS + 1,)), dma((STEPS + 1,)),
            dma((STEPS, 3)), dma((STEPS, 3)),
            dma((STEPS, 3, 4)), dma((STEPS, 3, 4)),
            dma((STEPS, 3, 2)), dma((STEPS, 3, 2)),
            dma((STEPS, 3)), dma((STEPS, 3)),
            dma((STEPS,)), dma((STEPS,)),
            dma((STEPS,)), dma((STEPS,)),
            dma((STEPS, 3)), dma((STEPS, 3)),
        ],
        compiler_params=pltpu.CompilerParams(
            collective_id=0, has_side_effects=True, vmem_limit_bytes=60 * 2**20
        ),
        cost_estimate=pl.CostEstimate(
            flops=STEPS * 3 * 2 * 512 * TILE**3, bytes_accessed=2 * SLOTS * TILE * TILE * 2, transcendentals=0
        ),
    )(users, items, coords, counts, ratings, weights)


def solution(mesh):
    return jax.shard_map(
        per_device,
        mesh=mesh,
        in_specs=(
            P(("users", "items"), None),
            P(("items", "users"), None),
            P("users", "items", None, None),
            P("users", "items"),
            P("users", "items", None, None, None),
            P("users", "items", None, None, None),
        ),
        out_specs=(P(("users", "items"), None), P(("items", "users"), None)),
        check_vma=False,
    )
```

profile of v0, /device:TPU:0, one launch (start us, length us, event | category | flops | bytes accessed | tf_op | source)
XLA Modules:
  0.0 86.3 jit_solution(6199895581342926012)
XLA Ops:
  1.3 1.5 %copy.8.coords_ref = s32[1,1,256,2]{3,2,1,0:T(8,128)} copy(s32[1,1,256,2]{2,3,1,0:T(2,128)} %param.8) | data formatting | bytes 4096 | tf_op args[2]
  2.8 80.4 %factorize.1 = (f32[128,128]{1,0:T(8,128)}, f32[512,128]{1,0:T(8,128)}) custom-call(f32[128,128]{1,0:T(8,128)} %users_ref.1, f32[512,128]{1,0:T(8,128)} %items_ref.1, s32[1,1,256,2]{3,2,1,0:T(8,128)} %copy.8.coords_ref, s32[1,1]{1,0:T(1,128)S(6)} %copy.11.counts_ref, bf16[1,1,256,128,128]{4,3,2,1,0:T(8,128)(2,1)} %ratings_hbm.1, ...), custom_call_target="tpu_custom_call" | custom-call | flops 12884901888 | bytes 16777216 | tf_op jit(solution)/shard_map/factorize/pallas_call | solution.py:295
  83.1 1.5 %copy.12 = f32[128,128]{1,0:T(8,128)} copy(f32[128,128]{1,0:T(8,128)} %get-tuple-element.4) | data formatting | bytes 131072
  84.6 1.7 %copy.13 = f32[512,128]{1,0:T(8,128)} copy(f32[512,128]{1,0:T(8,128)} %get-tuple-element.5) | data formatting | bytes 524288
where the time goes:
time: 86.5 us; the launch traced here: 86.3 us
  Pallas kernels  80.4 us (93%)
  local copies, waits for them, and re-layouts  4.62 us (5%)
  between operations  1.29 us (1%)
    pallas_call x1, Pallas kernels, per_device(): pl.pallas_call(kernel, name='factorize', out_shape=(jax.ShapeDtypeStruct(...  80.4 us
    unnamed x3, local copies, waits for them, and re-layouts  4.62 us

commit v1 on v0

v1 whole, which is shorter than its diff:
```python
import functools

import jax
import jax.numpy as jnp
from jax import lax
from jax.experimental import pallas as pl
from jax.experimental.pallas import tpu as pltpu
from jax.sharding import PartitionSpec as P

BF = jnp.bfloat16
F32 = jnp.float32
MESH = pl.DeviceIdType.MESH

TILE = 128
RANK = 128
STEPS = 2
SLOTS = 256
ITEM_BLOCKS = 16
USER_RATE = 20.0 / 65536
ITEM_RATE = 20.0 / 16384
LATE = 7


def contract(a, b, da, db):
    return lax.dot_general(a, b, (((da,), (db,)), ((), ())), preferred_element_type=F32)


def kernel(
    users_hbm, items_hbm, coords_hbm, counts_ref, ratings_hbm, weights_hbm,
    new_users_hbm, new_items_hbm,
    ratings, weights, coords, table_v, table_s,
    user_tab, item_tab, user_pair, user_master, item_master,
    grad_send, grad_own, ring_far, near_send, near_own, ring_near, pair_send, pair_recv,
    item_grad, core_send, core_recv, item_sum, zl_send, zl_recv,
    load_sem, pair_ss, pair_rs, agn_ss, agn_rs, agf_ss, agf_rs, rsf_ss, rsf_rs,
    rsn_ss, rsn_rs, core_ss, core_rs, zl_ss, zl_rs, agi_ss, agi_rs,
):
    me_u = lax.axis_index("users")
    me_i = lax.axis_index("items")
    core = me_u % 2
    zlo = me_u // 2
    x = me_i // 8
    y = (me_i // 2) % 4
    zh = me_i % 2
    near = x + core * (y - x)
    far = y + core * (x - y)
    near_stride = 8 - 6 * core
    far_stride = 2 + 6 * core

    def near_peer(r):
        return (me_u, me_i + ((near + r) % 4 - near) * near_stride)

    def far_peer(r):
        return (me_u, me_i + ((far + r) % 4 - far) * far_stride)

    pair_peer = (me_u, me_i + 1 - 2 * zh)
    core_peer = (me_u + 1 - 2 * core, me_i)
    zlo_peer = (me_u + 2 - 4 * zlo, me_i)

    def remote(src, dst, ss, rs, peer):
        return pltpu.make_async_remote_copy(
            src_ref=src, dst_ref=dst, send_sem=ss, recv_sem=rs, device_id=peer, device_id_type=MESH
        )

    load_items = pltpu.make_async_copy(items_hbm, item_master, load_sem.at[0])
    load_users = pltpu.make_async_copy(users_hbm, user_master.at[zh], load_sem.at[1])
    load_coords = pltpu.make_async_copy(coords_hbm.at[0, 0], coords, load_sem.at[2])
    load_items.start()
    load_users.start()
    load_coords.start()
    loads = (
        pltpu.make_async_copy(ratings_hbm.at[0, 0], ratings.at[pl.ds(0, SLOTS)], load_sem.at[3]),
        pltpu.make_async_copy(weights_hbm.at[0, 0], weights.at[pl.ds(0, SLOTS)], load_sem.at[4]),
    )
    for copy in loads:
        copy.start()
    to_scalars = pltpu.make_async_copy(table_v, table_s, load_sem.at[5])
    store_items = pltpu.make_async_copy(item_master, new_items_hbm, load_sem.at[6])
    store_users = pltpu.make_async_copy(user_pair, new_users_hbm, load_sem.at[7])

    peers = [near_peer(r) for r in (1, 2, 3)] + [far_peer(r) for r in (1, 2, 3)]
    peers += [pair_peer, core_peer, zlo_peer]
    barrier = pltpu.get_barrier_semaphore()
    for peer in peers:
        pl.semaphore_signal(barrier, inc=1, device_id=peer, device_id_type=MESH)
    pl.semaphore_wait(barrier, len(peers))

    def pair_rows():
        return remote(users_hbm, user_pair, pair_ss.at[0, 0], pair_rs.at[0, 0], pair_peer)

    def pair_sums(z):
        return remote(
            pair_send.at[0, z], pair_recv.at[0, z], pair_ss.at[1, z], pair_rs.at[1, z], pair_peer
        )

    def pair_last():
        return remote(
            pair_send.at[1, 1 - zh], pair_recv.at[1, 1 - zh], pair_ss.at[0, 1], pair_rs.at[0, 1], pair_peer
        )

    def gather_near(step, r, z):
        piece = user_tab.at[step, far, z, near]
        return remote(
            piece, piece, agn_ss.at[step, r - 1, z], agn_rs.at[step, r - 1, z], near_peer(r)
        )

    def gather_far(step, r, z):
        piece = user_tab.at[step, far, z]
        return remote(piece, piece, agf_ss.at[step, r - 1, z], agf_rs.at[step, r - 1, z], far_peer(r))

    def reduce_far(step, r, z):
        return remote(
            grad_send.at[step, r - 1, z], ring_far.at[step, r - 1, z],
            rsf_ss.at[step, r - 1, z], rsf_rs.at[step, r - 1, z], far_peer(r),
        )

    def reduce_near(step, r, z):
        return remote(
            near_send.at[step, z, (near + r) % 4], ring_near.at[step, z, r - 1],
            rsn_ss.at[step, r - 1, z], rsn_rs.at[step, r - 1, z], near_peer(r),
        )

    def reduce_core(step):
        return remote(core_send.at[step], core_recv.at[step], core_ss.at[step], core_rs.at[step], core_peer)

    def reduce_zlo(step):
        return remote(zl_send.at[step], zl_recv.at[step], zl_ss.at[step], zl_rs.at[step], zlo_peer)

    def gather_items(step, k):
        quarter = me_u if k < 2 else me_u + 2 - 4 * zlo
        piece = item_tab.at[step, quarter]
        return remote(
            piece, piece, agi_ss.at[step, k], agi_rs.at[step, k], zlo_peer if k == 0 else core_peer
        )

    def send_users(step, z):
        user_tab[step, far, z, near] = user_master[z].astype(BF)
        for r in (2, 1, 3):
            gather_near(step, r, z).start()

    def forward_users(step, z):
        for r in (1, 3, 2):
            gather_near(step, r, z).wait_recv()
        for r in (3, 2, 1):
            gather_far(step, r, z).start()

    def send_items(step):
        item_tab[step, me_u] = item_master[...].astype(BF)
        gather_items(step, 0).start()
        gather_items(step, 1).start()

    def sum_far(step, z):
        for r in (1, 2, 3):
            reduce_far(step, r, z).wait_recv()
        total = grad_own[z]
        for r in range(3):
            total = total + ring_far[step, r, z].astype(F32)
        near_own[z] = total.reshape(4, TILE, RANK)
        near_send[step, z] = total.astype(BF).reshape(4, TILE, RANK)
        for r in (2, 1, 3):
            reduce_near(step, r, z).start()

    def sum_near(step, z):
        for r in (1, 3, 2):
            reduce_near(step, r, z).wait_recv()
        total = near_own[z, near]
        for r in range(3):
            total = total + ring_near[step, z, r].astype(F32)
        near_own[z, near] = total
        pair_send[step, z] = total.astype(BF)

    def update_users(z):
        pair_sums(z).wait_recv()
        both = pair_send[0, z].astype(F32) + pair_recv[0, z].astype(F32)
        user_master[z] = user_master[z] - USER_RATE * both

    pair_rows().start()
    load_items.wait()
    send_items(0)

    load_coords.wait()
    cell = coords[0:1] * ITEM_BLOCKS + coords[1:2]
    cell = jnp.where(lax.broadcasted_iota(jnp.int32, (1, SLOTS), 1) < counts_ref[0, 0], cell, -1)
    cell = jnp.broadcast_to(cell, (8, SLOTS)).T[:, 0:1]
    slot = lax.broadcasted_iota(jnp.int32, (SLOTS, 512), 0)
    hit = cell == lax.broadcasted_iota(jnp.int32, (SLOTS, 512), 1)
    table_v[...] = SLOTS + jnp.sum(jnp.where(hit, slot - SLOTS, 0), axis=0, keepdims=True)
    to_scalars.start()
    ratings[SLOTS] = jnp.zeros((TILE, TILE), BF)
    weights[SLOTS] = jnp.zeros((TILE, TILE), BF)

    load_users.wait()
    pair_rows().wait_recv()
    user_master[1 - zh] = user_pair[...]
    for z in range(2):
        send_users(0, z)
    gather_items(0, 0).wait_recv()
    gather_items(0, 2).start()
    for z in range(2):
        forward_users(0, z)
    to_scalars.wait()
    gather_items(0, 1).wait_recv()
    gather_items(0, 2).wait_recv()
    for copy in loads:
        copy.wait()

    for step in range(STEPS):
        last = step + 1 == STEPS
        item_grad[...] = jnp.zeros_like(item_grad)

        def part(c, carry):
            z = c // 4
            rel = (c % 4 + z) % 4
            chunk = (far + rel) % 4

            if step > 0:
                @pl.when(c == 1)
                def _():
                    forward_users(step, 1)

            @pl.when(c == LATE)
            def _():
                sum_far(step, 0)

            @pl.when(rel > 0)
            def _():
                gather_far(step, 4 - rel, z).wait_recv()

            u = user_tab[step, chunk, z].reshape(4 * TILE, RANK)
            v = item_tab[step].reshape(ITEM_BLOCKS * TILE, RANK)
            scores = contract(u, v, 1, 1)
            rows = []
            for a in range(4):
                block = a * near_stride + chunk * far_stride + z
                cols = []
                for b in range(ITEM_BLOCKS):
                    k = table_s[0, block * ITEM_BLOCKS + b]
                    score = scores[a * TILE:(a + 1) * TILE, b * TILE:(b + 1) * TILE]
                    err = weights[k].astype(F32) * (score - ratings[k].astype(F32))
                    cols.append(err.astype(BF))
                rows.append(jnp.concatenate(cols, axis=1))
            errors = jnp.concatenate(rows, axis=0)
            user_part = contract(errors, v, 1, 0)
            item_part = contract(u, errors, 0, 0)
            for q in range(4):
                item_grad[q] += item_part[:, q * 512:(q + 1) * 512]

            @pl.when(rel == 0)
            def _():
                grad_own[z] = user_part

            @pl.when(rel > 0)
            def _():
                grad_send[step, rel - 1, z] = user_part.astype(BF)
                reduce_far(step, rel, z).start()

            return carry

        lax.fori_loop(0, 8, part, 0)

        for k in range(2):
            core_send[step, k] = item_grad[2 * k + 1 - core].astype(BF)
        reduce_core(step).start()

        sum_near(step, 0)
        if not last:
            pair_sums(0).start()

        reduce_core(step).wait_recv()
        zl_send[step] = (item_grad[2 - 2 * zlo + core] + core_recv[step, 1 - zlo].astype(F32)).astype(BF)
        reduce_zlo(step).start()
        item_sum[...] = (item_grad[2 * zlo + core] + core_recv[step, zlo].astype(F32)).T

        sum_far(step, 1)
        if not last:
            update_users(0)
            send_users(step + 1, 0)
            sum_near(step, 1)
            pair_sums(1).start()

        reduce_zlo(step).wait_recv()
        item_total = item_sum[...] + zl_recv[step].astype(F32).T
        item_master[...] = item_master[...] - ITEM_RATE * item_total
        if not last:
            send_items(step + 1)
            forward_users(step + 1, 0)
            update_users(1)
            send_users(step + 1, 1)
            gather_items(step + 1, 0).wait_recv()
            gather_items(step + 1, 2).start()
            gather_items(step + 1, 1).wait_recv()
            gather_items(step + 1, 2).wait_recv()
        else:
            store_items.start()
            sum_near(step, 1)
            pair_last().start()
            pair_last().wait_recv()
            mine = near_own[zh, near] + pair_recv[1, zh].astype(F32)
            user_pair[...] = user_master[zh] - USER_RATE * mine
            store_users.start()

    for step in range(STEPS):
        for z in range(2):
            for r in (1, 2, 3):
                gather_near(step, r, z).wait_send()
                gather_far(step, r, z).wait_send()
                reduce_far(step, r, z).wait_send()
                reduce_near(step, r, z).wait_send()
        reduce_core(step).wait_send()
        reduce_zlo(step).wait_send()
        for k in range(3):
            gather_items(step, k).wait_send()
    pair_rows().wait_send()
    pair_sums(0).wait_send()
    pair_sums(1).wait_send()
    pair_last().wait_send()
    store_items.wait()
    store_users.wait()


def per_device(users, items, coords, counts, ratings, weights):
    hbm = pl.BlockSpec(memory_space=pl.ANY)
    dma = pltpu.SemaphoreType.DMA
    return pl.pallas_call(
        kernel,
        name="factorize",
        out_shape=(
            jax.ShapeDtypeStruct(users.shape, F32),
            jax.ShapeDtypeStruct(items.shape, F32),
        ),
        in_specs=[hbm, hbm, hbm, pl.BlockSpec(memory_space=pltpu.SMEM), hbm, hbm],
        out_specs=(hbm, hbm),
        scratch_shapes=[
            pltpu.VMEM((SLOTS + 1, TILE, TILE), BF),
            pltpu.VMEM((SLOTS + 1, TILE, TILE), BF),
            pltpu.VMEM((2, SLOTS), jnp.int32),
            pltpu.VMEM((1, 512), jnp.int32),
            pltpu.SMEM((1, 512), jnp.int32),
            pltpu.VMEM((STEPS, 4, 2, 4, TILE, RANK), BF),
            pltpu.VMEM((STEPS, 4, 512, RANK), BF),
            pltpu.VMEM((TILE, RANK), F32),
            pltpu.VMEM((2, TILE, RANK), F32),
            pltpu.VMEM((512, RANK), F32),
            pltpu.VMEM((STEPS, 3, 2, 512, RANK), BF),
            pltpu.VMEM((2, 512, RANK), F32),
            pltpu.VMEM((STEPS, 3, 2, 512, RANK), BF),
            pltpu.VMEM((STEPS, 2, 4, TILE, RANK), BF),
            pltpu.VMEM((2, 4, TILE, RANK), F32),
            pltpu.VMEM((STEPS, 2, 3, TILE, RANK), BF),
            pltpu.VMEM((STEPS, 2, TILE, RANK), BF),
            pltpu.VMEM((STEPS, 2, TILE, RANK), BF),
            pltpu.VMEM((4, RANK, 512), F32),
            pltpu.VMEM((STEPS, 2, RANK, 512), BF),
            pltpu.VMEM((STEPS, 2, RANK, 512), BF),
            pltpu.VMEM((512, RANK), F32),
            pltpu.VMEM((STEPS, RANK, 512), BF),
            pltpu.VMEM((STEPS, RANK, 512), BF),
            dma((8,)),
            dma((2, 2)), dma((2, 2)),
            dma((STEPS, 3, 2)), dma((STEPS, 3, 2)),
            dma((STEPS, 3, 2)), dma((STEPS, 3, 2)),
            dma((STEPS, 3, 2)), dma((STEPS, 3, 2)),
            dma((STEPS, 3, 2)), dma((STEPS, 3, 2)),
            dma((STEPS,)), dma((STEPS,)),
            dma((STEPS,)), dma((STEPS,)),
            dma((STEPS, 3)), dma((STEPS, 3)),
        ],
        compiler_params=pltpu.CompilerParams(
            collective_id=0, has_side_effects=True, vmem_limit_bytes=60 * 2**20
        ),
        cost_estimate=pl.CostEstimate(
            flops=STEPS * 3 * 2 * 512 * TILE**3, bytes_accessed=2 * SLOTS * TILE * TILE * 2, transcendentals=0
        ),
    )(users, items, jnp.swapaxes(coords, 2, 3), counts, ratings, weights)


def solution(mesh):
    return jax.shard_map(
        per_device,
        mesh=mesh,
        in_specs=(
            P(("users", "items"), None),
            P(("items", "users"), None),
            P("users", "items", None, None),
            P("users", "items"),
            P("users", "items", None, None, None),
            P("users", "items", None, None, None),
        ),
        out_specs=(P(("users", "items"), None), P(("items", "users"), None)),
        check_vma=False,
    )
```

time: 86.5 us -> 78 us (0.902)
  Pallas kernels: 80.4 us -> 73.2 us
  local copies, waits for them, and re-layouts: 4.62 us -> 3.14 us
    pallas_call x1, Pallas kernels: 80.4 us -> 73.2 us  [per_device(): pl.pallas_call(kernel, name='factorize', out_shape=(jax.ShapeDtypeStruct(...]
    unnamed x3 -> x2, local copies, waits for them, and re-layouts: 4.62 us -> 3.14 us
where the time goes in v1:
time: 78 us; the launch traced here: 77.6 us
  Pallas kernels  73.2 us (94%)
  local copies, waits for them, and re-layouts  3.14 us (4%)
  between operations  1.29 us (2%)
    pallas_call x1, Pallas kernels, per_device(): pl.pallas_call(kernel, name='factorize', out_shape=(jax.ShapeDtypeStruct(...  73.2 us
    unnamed x2, local copies, waits for them, and re-layouts  3.14 us

profile of v1, /device:TPU:0, one launch (start us, length us, event | category | flops | bytes accessed | tf_op | source)
XLA Modules:
  0.0 77.6 jit_solution(12389535334205645234)
XLA Ops:
  1.3 73.2 %factorize.1 = (f32[128,128]{1,0:T(8,128)}, f32[512,128]{1,0:T(8,128)}) custom-call(f32[128,128]{1,0:T(8,128)} %users_hbm.1, f32[512,128]{1,0:T(8,128)} %items_hbm.1, s32[1,1,2,256]{3,2,1,0:T(2,128)} %bitcast.1, s32[1,1]{1,0:T(1,128)S(6)} %copy.10.counts_ref, bf16[1,1,256,128,128]{4,3,2,1,0:T(8,128)(2,1)} %ratings_hbm.1, ...), custom_call_target="tpu_custom_call" | custom-call | flops 12884901888 | bytes 16777216 | tf_op jit(solution)/shard_map/factorize/pallas_call | solution.py:324
  74.4 1.5 %copy.11 = f32[128,128]{1,0:T(8,128)} copy(f32[128,128]{1,0:T(8,128)} %get-tuple-element.4) | data formatting | bytes 131072
  75.9 1.7 %copy.12 = f32[512,128]{1,0:T(8,128)} copy(f32[512,128]{1,0:T(8,128)} %get-tuple-element.5) | data formatting | bytes 524288

commit v2 on v1

--- a/solution.py
+++ b/solution.py
@@ -18,7 +18,8 @@
 ITEM_BLOCKS = 16
 USER_RATE = 20.0 / 65536
 ITEM_RATE = 20.0 / 16384
-LATE = 7
+LATE = (7, 7)
+OWN_FIRST = True
 
 
 def contract(a, b, da, db):
@@ -30,10 +31,10 @@
     new_users_hbm, new_items_hbm,
     ratings, weights, coords, table_v, table_s,
     user_tab, item_tab, user_pair, user_master, item_master,
-    grad_send, grad_own, ring_far, near_send, near_own, ring_near, pair_send, pair_recv,
+    grad_send, grad_own, ring_far, near_send, near_own, ring_near, ring_cross, pair_send, pair_recv,
     item_grad, core_send, core_recv, item_sum, zl_send, zl_recv,
     load_sem, pair_ss, pair_rs, agn_ss, agn_rs, agf_ss, agf_rs, rsf_ss, rsf_rs,
-    rsn_ss, rsn_rs, core_ss, core_rs, zl_ss, zl_rs, agi_ss, agi_rs,
+    rsn_ss, rsn_rs, rsc_ss, rsc_rs, core_ss, core_rs, zl_ss, zl_rs, agi_ss, agi_rs,
 ):
     me_u = lax.axis_index("users")
     me_i = lax.axis_index("items")
@@ -53,7 +54,10 @@
     def far_peer(r):
         return (me_u, me_i + ((far + r) % 4 - far) * far_stride)
 
-    pair_peer = (me_u, me_i + 1 - 2 * zh)
+    def cross_peer(r):
+        return (me_u, me_i + ((near + r) % 4 - near) * near_stride + 1 - 2 * zh)
+
+    pair_peer = cross_peer(0)
     core_peer = (me_u + 1 - 2 * core, me_i)
     zlo_peer = (me_u + 2 - 4 * zlo, me_i)
 
@@ -79,7 +83,7 @@
     store_users = pltpu.make_async_copy(user_pair, new_users_hbm, load_sem.at[7])
 
     peers = [near_peer(r) for r in (1, 2, 3)] + [far_peer(r) for r in (1, 2, 3)]
-    peers += [pair_peer, core_peer, zlo_peer]
+    peers += [cross_peer(r) for r in range(4)] + [core_peer, zlo_peer]
     barrier = pltpu.get_barrier_semaphore()
     for peer in peers:
         pl.semaphore_signal(barrier, inc=1, device_id=peer, device_id_type=MESH)
@@ -93,11 +97,6 @@
             pair_send.at[0, z], pair_recv.at[0, z], pair_ss.at[1, z], pair_rs.at[1, z], pair_peer
         )
 
-    def pair_last():
-        return remote(
-            pair_send.at[1, 1 - zh], pair_recv.at[1, 1 - zh], pair_ss.at[0, 1], pair_rs.at[0, 1], pair_peer
-        )
-
     def gather_near(step, r, z):
         piece = user_tab.at[step, far, z, near]
         return remote(
@@ -116,8 +115,13 @@
 
     def reduce_near(step, r, z):
         return remote(
-            near_send.at[step, z, (near + r) % 4], ring_near.at[step, z, r - 1],
+            near_send.at[step, z if step + 1 < STEPS else zh, (near + r) % 4], ring_near.at[step, z, r - 1],
             rsn_ss.at[step, r - 1, z], rsn_rs.at[step, r - 1, z], near_peer(r),
+        )
+
+    def reduce_cross(r, z):
+        return remote(
+            near_send.at[1, z, (near + r) % 4], ring_cross.at[r], rsc_ss.at[r], rsc_rs.at[r], cross_peer(r)
         )
 
     def reduce_core(step):
@@ -157,8 +161,19 @@
             total = total + ring_far[step, r, z].astype(F32)
         near_own[z] = total.reshape(4, TILE, RANK)
         near_send[step, z] = total.astype(BF).reshape(4, TILE, RANK)
-        for r in (2, 1, 3):
-            reduce_near(step, r, z).start()
+        if step + 1 < STEPS:
+            for r in (2, 1, 3):
+                reduce_near(step, r, z).start()
+        else:
+            @pl.when(zh == z)
+            def _():
+                for r in (2, 1, 3):
+                    reduce_near(step, r, 0).start()
+
+            @pl.when(zh != z)
+            def _():
+                for r in (2, 1, 3, 0):
+                    reduce_cross(r, z).start()
 
     def sum_near(step, z):
         for r in (1, 3, 2):
@@ -209,8 +224,12 @@
         item_grad[...] = jnp.zeros_like(item_grad)
 
         def part(c, carry):
-            z = c // 4
-            rel = (c % 4 + z) % 4
+            if step == 0 and OWN_FIRST:
+                z = jnp.where(c < 2, c, (c - 2) // 3)
+                rel = jnp.where(c < 2, 0, (c - 2) % 3 + 1)
+            else:
+                z = c // 4
+                rel = (c % 4 + z) % 4
             chunk = (far + rel) % 4
 
             if step > 0:
@@ -218,7 +237,7 @@
                 def _():
                     forward_users(step, 1)
 
-            @pl.when(c == LATE)
+            @pl.when(c == LATE[step])
             def _():
                 sum_far(step, 0)
 
@@ -262,14 +281,14 @@
             core_send[step, k] = item_grad[2 * k + 1 - core].astype(BF)
         reduce_core(step).start()
 
-        sum_near(step, 0)
-        if not last:
-            pair_sums(0).start()
-
         reduce_core(step).wait_recv()
         zl_send[step] = (item_grad[2 - 2 * zlo + core] + core_recv[step, 1 - zlo].astype(F32)).astype(BF)
         reduce_zlo(step).start()
         item_sum[...] = (item_grad[2 * zlo + core] + core_recv[step, zlo].astype(F32)).T
+
+        if not last:
+            sum_near(step, 0)
+            pair_sums(0).start()
 
         sum_far(step, 1)
         if not last:
@@ -277,7 +296,6 @@
             send_users(step + 1, 0)
             sum_near(step, 1)
             pair_sums(1).start()
-
         reduce_zlo(step).wait_recv()
         item_total = item_sum[...] + zl_recv[step].astype(F32).T
         item_master[...] = item_master[...] - ITEM_RATE * item_total
@@ -292,10 +310,13 @@
             gather_items(step + 1, 2).wait_recv()
         else:
             store_items.start()
-            sum_near(step, 1)
-            pair_last().start()
-            pair_last().wait_recv()
-            mine = near_own[zh, near] + pair_recv[1, zh].astype(F32)
+            mine = near_own[zh, near]
+            for r in (1, 3, 2):
+                reduce_near(step, r, 0).wait_recv()
+                mine = mine + ring_near[step, 0, r - 1].astype(F32)
+            for r in (0, 1, 3, 2):
+                reduce_cross(r, 1 - zh).wait_recv()
+                mine = mine + ring_cross[r].astype(F32)
             user_pair[...] = user_master[zh] - USER_RATE * mine
             store_users.start()
 
@@ -305,7 +326,8 @@
                 gather_near(step, r, z).wait_send()
                 gather_far(step, r, z).wait_send()
                 reduce_far(step, r, z).wait_send()
-                reduce_near(step, r, z).wait_send()
+                if step + 1 < STEPS or z == 0:
+                    reduce_near(step, r, z).wait_send()
         reduce_core(step).wait_send()
         reduce_zlo(step).wait_send()
         for k in range(3):
@@ -313,15 +335,21 @@
     pair_rows().wait_send()
     pair_sums(0).wait_send()
     pair_sums(1).wait_send()
-    pair_last().wait_send()
+    for r in range(4):
+        reduce_cross(r, 1 - zh).wait_send()
     store_items.wait()
     store_users.wait()
+
+
+def finish(a_ref, b_ref, c_ref, d_ref):
+    c_ref[...] = a_ref[...]
+    d_ref[...] = b_ref[...]
 
 
 def per_device(users, items, coords, counts, ratings, weights):
     hbm = pl.BlockSpec(memory_space=pl.ANY)
     dma = pltpu.SemaphoreType.DMA
-    return pl.pallas_call(
+    users_out, items_out = pl.pallas_call(
         kernel,
         name="factorize",
         out_shape=(
@@ -347,6 +375,7 @@
             pltpu.VMEM((STEPS, 2, 4, TILE, RANK), BF),
             pltpu.VMEM((2, 4, TILE, RANK), F32),
             pltpu.VMEM((STEPS, 2, 3, TILE, RANK), BF),
+            pltpu.VMEM((4, TILE, RANK), BF),
             pltpu.VMEM((STEPS, 2, TILE, RANK), BF),
             pltpu.VMEM((STEPS, 2, TILE, RANK), BF),
             pltpu.VMEM((4, RANK, 512), F32),
@@ -361,6 +390,7 @@
             dma((STEPS, 3, 2)), dma((STEPS, 3, 2)),
             dma((STEPS, 3, 2)), dma((STEPS, 3, 2)),
             dma((STEPS, 3, 2)), dma((STEPS, 3, 2)),
+            dma((4,)), dma((4,)),
             dma((STEPS,)), dma((STEPS,)),
             dma((STEPS,)), dma((STEPS,)),
             dma((STEPS, 3)), dma((STEPS, 3)),
@@ -372,6 +402,17 @@
             flops=STEPS * 3 * 2 * 512 * TILE**3, bytes_accessed=2 * SLOTS * TILE * TILE * 2, transcendentals=0
         ),
     )(users, items, jnp.swapaxes(coords, 2, 3), counts, ratings, weights)
+    vmem = pl.BlockSpec(memory_space=pltpu.VMEM)
+    return pl.pallas_call(
+        finish,
+        name="finish",
+        out_shape=(
+            jax.ShapeDtypeStruct(users.shape, F32),
+            jax.ShapeDtypeStruct(items.shape, F32),
+        ),
+        in_specs=[vmem, vmem],
+        out_specs=(vmem, vmem),
+    )(users_out, items_out)
 
 
 def solution(mesh):

time: 78 us -> 74.1 us (0.950)
  the two profiles are of different devices: /device:TPU:0 before, /device:TPU:1 now
where the time goes in v2:
time: 74.1 us; the launch traced here: 74 us
  Pallas kernels  72.7 us (98%)
  between operations  1.28 us (2%)
    pallas_call x1, Pallas kernels, per_device(): pl.pallas_call(kernel, name='factorize', out_shape=(jax.ShapeDtypeStruct(...  71 us
    pallas_call x1, Pallas kernels, per_device(): pl.pallas_call(finish, name='finish', out_shape=(jax.ShapeDtypeStruct(use...  1.72 us

profile of v2, /device:TPU:1, one launch (start us, length us, event | category | flops | bytes accessed | tf_op | source)
XLA Modules:
  0.0 74.0 jit_solution(7954485345197874088)
XLA Ops:
  1.3 71.0 %factorize.1 = (f32[128,128]{1,0:T(8,128)}, f32[512,128]{1,0:T(8,128)}) custom-call(f32[128,128]{1,0:T(8,128)} %users_hbm.1, f32[512,128]{1,0:T(8,128)} %items_hbm.1, s32[1,1,2,256]{3,2,1,0:T(2,128)} %bitcast.1, s32[1,1]{1,0:T(1,128)S(6)} %copy.8.counts_ref, bf16[1,1,256,128,128]{4,3,2,1,0:T(8,128)(2,1)} %ratings_hbm.1, ...), custom_call_target="tpu_custom_call" | custom-call | flops 12884901888 | bytes 16777216 | tf_op jit(solution)/shard_map/factorize/pallas_call | solution.py:352
  72.2 1.7 %finish.1 = (f32[128,128]{1,0:T(8,128)}, f32[512,128]{1,0:T(8,128)}) custom-call(f32[128,128]{1,0:T(8,128)} %get-tuple-element.4.a_ref, f32[512,128]{1,0:T(8,128)} %get-tuple-element.5.b_ref), custom_call_target="tpu_custom_call" | custom-call | tf_op jit(solution)/shard_map/finish/pallas_call | solution.py:406

commit v3 on v2

--- a/solution.py
+++ b/solution.py
@@ -31,10 +31,10 @@
     new_users_hbm, new_items_hbm,
     ratings, weights, coords, table_v, table_s,
     user_tab, item_tab, user_pair, user_master, item_master,
-    grad_send, grad_own, ring_far, near_send, near_own, ring_near, ring_cross, pair_send, pair_recv,
+    grad_send, grad_own, ring_far, near_send, near_own, ring_near, ring_cross, ring_both,
     item_grad, core_send, core_recv, item_sum, zl_send, zl_recv,
-    load_sem, pair_ss, pair_rs, agn_ss, agn_rs, agf_ss, agf_rs, rsf_ss, rsf_rs,
-    rsn_ss, rsn_rs, rsc_ss, rsc_rs, core_ss, core_rs, zl_ss, zl_rs, agi_ss, agi_rs,
+    load_sem, pair_ss, pair_rs, agn_ss, agn_rs, agf_ss, agf_rs, agb_ss, agb_rs, rsf_ss, rsf_rs,
+    rsn_ss, rsn_rs, rsc_ss, rsc_rs, rsb_ss, rsb_rs, core_ss, core_rs, zl_ss, zl_rs, agi_ss, agi_rs,
 ):
     me_u = lax.axis_index("users")
     me_i = lax.axis_index("items")
@@ -92,15 +92,31 @@
     def pair_rows():
         return remote(users_hbm, user_pair, pair_ss.at[0, 0], pair_rs.at[0, 0], pair_peer)
 
-    def pair_sums(z):
-        return remote(
-            pair_send.at[0, z], pair_recv.at[0, z], pair_ss.at[1, z], pair_rs.at[1, z], pair_peer
+    def reduce_both(z, w, r):
+        mine = zh * 4 + near
+        return remote(
+            near_send.at[0, z, (near + r) % 4], ring_both.at[z, mine],
+            rsb_ss.at[z, w * 4 + r], rsb_rs.at[z, mine], cross_peer(r) if w else near_peer(r),
+        )
+
+    def from_both(z, w, r):
+        source = (zh + w) % 2 * 4 + (near + 4 - r) % 4
+        return remote(
+            near_send.at[0, z, (near + r) % 4], ring_both.at[z, source],
+            rsb_ss.at[z, w * 4 + r], rsb_rs.at[z, source], cross_peer(r) if w else near_peer(r),
         )
 
     def gather_near(step, r, z):
         piece = user_tab.at[step, far, z, near]
         return remote(
             piece, piece, agn_ss.at[step, r - 1, z], agn_rs.at[step, r - 1, z], near_peer(r)
+        )
+
+    def gather_both(w, r):
+        piece = user_tab.at[0, far, zh, near]
+        k = w * 4 + r
+        return remote(
+            piece, piece, agb_ss.at[k], agb_rs.at[k], cross_peer(r) if w else near_peer(r)
         )
 
     def gather_far(step, r, z):
@@ -143,8 +159,20 @@
             gather_near(step, r, z).start()
 
     def forward_users(step, z):
-        for r in (1, 3, 2):
-            gather_near(step, r, z).wait_recv()
+        if step > 0:
+            for r in (1, 3, 2):
+                gather_near(step, r, z).wait_recv()
+        else:
+            @pl.when(zh == z)
+            def _():
+                for r in (1, 3, 2):
+                    gather_both(0, r).wait_recv()
+
+            @pl.when(zh != z)
+            def _():
+                for r in (0, 1, 3, 2):
+                    gather_both(1, r).wait_recv()
+
         for r in (3, 2, 1):
             gather_far(step, r, z).start()
 
@@ -162,8 +190,11 @@
         near_own[z] = total.reshape(4, TILE, RANK)
         near_send[step, z] = total.astype(BF).reshape(4, TILE, RANK)
         if step + 1 < STEPS:
+            ring_both[z, zh * 4 + near] = near_send[0, z, near]
+            for r in (2, 1, 3, 0):
+                reduce_both(z, 1, r).start()
             for r in (2, 1, 3):
-                reduce_near(step, r, z).start()
+                reduce_both(z, 0, r).start()
         else:
             @pl.when(zh == z)
             def _():
@@ -175,21 +206,22 @@
                 for r in (2, 1, 3, 0):
                     reduce_cross(r, z).start()
 
-    def sum_near(step, z):
+    def update_users(z):
         for r in (1, 3, 2):
-            reduce_near(step, r, z).wait_recv()
-        total = near_own[z, near]
-        for r in range(3):
-            total = total + ring_near[step, z, r].astype(F32)
-        near_own[z, near] = total
-        pair_send[step, z] = total.astype(BF)
-
-    def update_users(z):
-        pair_sums(z).wait_recv()
-        both = pair_send[0, z].astype(F32) + pair_recv[0, z].astype(F32)
-        user_master[z] = user_master[z] - USER_RATE * both
-
-    pair_rows().start()
+            from_both(z, 0, r).wait_recv()
+        for r in (0, 1, 3, 2):
+            from_both(z, 1, r).wait_recv()
+        total = ring_both[z, 0].astype(F32)
+        for k in range(1, 8):
+            total = total + ring_both[z, k].astype(F32)
+        user_master[z] = user_master[z] - USER_RATE * total
+
+    load_users.wait()
+    user_tab[0, far, zh, near] = user_master[zh].astype(BF)
+    for r in (2, 1, 3, 0):
+        gather_both(1, r).start()
+    for r in (2, 1, 3):
+        gather_both(0, r).start()
     load_items.wait()
     send_items(0)
 
@@ -204,15 +236,11 @@
     ratings[SLOTS] = jnp.zeros((TILE, TILE), BF)
     weights[SLOTS] = jnp.zeros((TILE, TILE), BF)
 
-    load_users.wait()
-    pair_rows().wait_recv()
-    user_master[1 - zh] = user_pair[...]
-    for z in range(2):
-        send_users(0, z)
     gather_items(0, 0).wait_recv()
     gather_items(0, 2).start()
     for z in range(2):
         forward_users(0, z)
+    pair_rows().start()
     to_scalars.wait()
     gather_items(0, 1).wait_recv()
     gather_items(0, 2).wait_recv()
@@ -286,16 +314,12 @@
         reduce_zlo(step).start()
         item_sum[...] = (item_grad[2 * zlo + core] + core_recv[step, zlo].astype(F32)).T
 
-        if not last:
-            sum_near(step, 0)
-            pair_sums(0).start()
-
         sum_far(step, 1)
         if not last:
+            pair_rows().wait_recv()
+            user_master[1 - zh] = user_pair[...]
             update_users(0)
             send_users(step + 1, 0)
-            sum_near(step, 1)
-            pair_sums(1).start()
         reduce_zlo(step).wait_recv()
         item_total = item_sum[...] + zl_recv[step].astype(F32).T
         item_master[...] = item_master[...] - ITEM_RATE * item_total
@@ -323,18 +347,24 @@
     for step in range(STEPS):
         for z in range(2):
             for r in (1, 2, 3):
-                gather_near(step, r, z).wait_send()
+                if step > 0:
+                    gather_near(step, r, z).wait_send()
                 gather_far(step, r, z).wait_send()
                 reduce_far(step, r, z).wait_send()
-                if step + 1 < STEPS or z == 0:
+                if step + 1 < STEPS:
+                    reduce_both(z, 0, r).wait_send()
+                elif z == 0:
                     reduce_near(step, r, z).wait_send()
         reduce_core(step).wait_send()
         reduce_zlo(step).wait_send()
         for k in range(3):
             gather_items(step, k).wait_send()
     pair_rows().wait_send()
-    pair_sums(0).wait_send()
-    pair_sums(1).wait_send()
+    for k in range(1, 8):
+        gather_both(k // 4, k % 4).wait_send()
+    for z in range(2):
+        for r in range(4):
+            reduce_both(z, 1, r).wait_send()
     for r in range(4):
         reduce_cross(r, 1 - zh).wait_send()
     store_items.wait()
@@ -376,8 +406,7 @@
             pltpu.VMEM((2, 4, TILE, RANK), F32),
             pltpu.VMEM((STEPS, 2, 3, TILE, RANK), BF),
             pltpu.VMEM((4, TILE, RANK), BF),
-            pltpu.VMEM((STEPS, 2, TILE, RANK), BF),
-            pltpu.VMEM((STEPS, 2, TILE, RANK), BF),
+            pltpu.VMEM((2, 8, TILE, RANK), BF),
             pltpu.VMEM((4, RANK, 512), F32),
             pltpu.VMEM((STEPS, 2, RANK, 512), BF),
             pltpu.VMEM((STEPS, 2, RANK, 512), BF),
@@ -388,9 +417,11 @@
             dma((2, 2)), dma((2, 2)),
             dma((STEPS, 3, 2)), dma((STEPS, 3, 2)),
             dma((STEPS, 3, 2)), dma((STEPS, 3, 2)),
+            dma((8,)), dma((8,)),
             dma((STEPS, 3, 2)), dma((STEPS, 3, 2)),
             dma((STEPS, 3, 2)), dma((STEPS, 3, 2)),
             dma((4,)), dma((4,)),
+            dma((2, 8)), dma((2, 8)),
             dma((STEPS,)), dma((STEPS,)),
             dma((STEPS,)), dma((STEPS,)),
             dma((STEPS, 3)), dma((STEPS, 3)),

time: 74.1 us -> 69.6 us (0.939)
  the two profiles are of different devices: /device:TPU:1 before, /device:TPU:0 now
where the time goes in v3:
time: 69.6 us; the launch traced here: 69.5 us
  Pallas kernels  68.2 us (98%)
  between operations  1.28 us (2%)
    pallas_call x1, Pallas kernels, per_device(): pl.pallas_call(kernel, name='factorize', out_shape=(jax.ShapeDtypeStruct(...  66.5 us
    pallas_call x1, Pallas kernels, per_device(): pl.pallas_call(finish, name='finish', out_shape=(jax.ShapeDtypeStruct(use...  1.72 us

profile of v3, /device:TPU:0, one launch (start us, length us, event | category | flops | bytes accessed | tf_op | source)
XLA Modules:
  0.0 69.5 jit_solution(14867982091879369888)
XLA Ops:
  1.3 66.5 %factorize.1 = (f32[128,128]{1,0:T(8,128)}, f32[512,128]{1,0:T(8,128)}) custom-call(f32[128,128]{1,0:T(8,128)} %users_hbm.1, f32[512,128]{1,0:T(8,128)} %items_hbm.1, s32[1,1,2,256]{3,2,1,0:T(2,128)} %bitcast.1, s32[1,1]{1,0:T(1,128)S(6)} %copy.8.counts_ref, bf16[1,1,256,128,128]{4,3,2,1,0:T(8,128)(2,1)} %ratings_hbm.1, ...), custom_call_target="tpu_custom_call" | custom-call | flops 12884901888 | bytes 16777216 | tf_op jit(solution)/shard_map/factorize/pallas_call | solution.py:382
  67.8 1.7 %finish.1 = (f32[128,128]{1,0:T(8,128)}, f32[512,128]{1,0:T(8,128)}) custom-call(f32[128,128]{1,0:T(8,128)} %get-tuple-element.4.a_ref, f32[512,128]{1,0:T(8,128)} %get-tuple-element.5.b_ref), custom_call_target="tpu_custom_call" | custom-call | tf_op jit(solution)/shard_map/finish/pallas_call | solution.py:437
